TPU v7x, 32 devices: a whole 2x2x4 slice. The times are simulated.
32 devices in a mesh: dom: 8 (over y, x, core), grp: 4 (over z).
Axes of the slice: x: 2, y: 2, z: 4, core: 2. Of those that a mesh axis runs over, the one named last changes fastest.
Arguments:
- features: bfloat16 [65536, 256], P(('dom', 'grp')), may hold values from -6 to 6
- edge_src: int32 [524288], P(('dom', 'grp')), may hold values from 0 to 2303, as said below
- edge_dst: int32 [524288], P(('dom', 'grp')), may hold values from 0 to 2047, as said below
- edge_count: int32 [32], P(('dom', 'grp')), may hold values from 4096 to 16384, as said below
- halo_index: int32 [32, 32, 8], P(('dom', 'grp')), may hold values from 0 to 2047
- request_rows: int32 [32, 32, 16], P(('dom', 'grp')), may hold values from 0 to 2047, as said below
- pair_ends: int32 [65536, 2], P(('dom', 'grp')), may hold values from 0 to 511
- labels: int32 [65536], P(('dom', 'grp')), may hold values 0 or 1
- pair_weight: float32 [65536], P(('dom', 'grp')), may hold values from 0.25 to 4
- w_self: bfloat16 [256, 256], replicated, may hold values from -0.375 to 0.375
- w_neigh: bfloat16 [256, 256], replicated, may hold values from -0.375 to 0.375
- w_hidden: bfloat16 [512, 256], replicated, may hold values from -0.25 to 0.25
- b_hidden: float32 [256], replicated, may hold values from -3 to 3
- w_out: float32 [256], replicated, may hold values from -0.375 to 0.375
Outputs:
- logits: float32 [65536], P(('dom', 'grp'))
- grad_features: float32 [65536, 256], P(('dom', 'grp'))
- grad_w_self: float32 [256, 256], replicated
- grad_w_neigh: float32 [256, 256], replicated
- grad_w_hidden: float32 [512, 256], replicated
- grad_b_hidden: float32 [256], replicated
- grad_w_out: float32 [256], replicated
Inputs may be any that keep to these rules, and one draw needn't show every extreme that they name: `edge_src`: a row of the partition's own table. `edge_dst`: a local node of the partition; slots at or past edge_count are not live and hold arbitrary values. `edge_count`: some partition has exactly 16384 live slots. `halo_index`: local rows of the sending partition; 8 to every partition, itself included. `request_rows`: local rows of the owning partition, distinct and increasing within each list of 16. `pair_ends`: rows of the shard's own received rows.
All inputs are finite; a program needn't handle non-finite values. No bound on the sum of `labels` on one device may be relied on, other than what follows from the above.
Results may differ from a plain program's by a relative error of at most 0.02.
The roundings to bfloat16 on the way count: a program that leaves them out, or rounds other values in their place, can miss the bound.
Values may be sent and summed in bfloat16 or wider, within the bound.
A program may use at most 192 MiB of HBM per device.

v0:
```python
import jax
import jax.numpy as jnp
from jax import lax
from jax.sharding import PartitionSpec as P


def contract_rows(left, right):
    return lax.dot_general(
        left,
        right,
        (((0,), (0,)), ((), ())),
        precision=lax.Precision.HIGHEST,
        preferred_element_type=jnp.float32,
    )


def per_device(
    features,
    edge_src,
    edge_dst,
    edge_count,
    halo_index,
    request_rows,
    pair_ends,
    labels,
    pair_weight,
    w_self,
    w_neigh,
    w_hidden,
    b_hidden,
    w_out,
):
    node_rows, feat_width = features.shape
    dom_count = lax.axis_size("dom")
    grp_count = lax.axis_size("grp")
    peer_count = dom_count * grp_count
    halo_len = halo_index.shape[2]
    outgoing = features[halo_index[0]]
    arrived = lax.all_to_all(
        lax.all_to_all(
            outgoing.reshape(dom_count, grp_count, halo_len, feat_width),
            "dom",
            split_axis=0,
            concat_axis=0,
            tiled=True,
        ),
        "grp",
        split_axis=1,
        concat_axis=1,
        tiled=True,
    )
    row_table = jnp.concatenate(
        [features, arrived.reshape(peer_count * halo_len, feat_width)], axis=0
    )
    table_rows = row_table.shape[0]
    slot_total = edge_src.shape[0]
    alive_slot = jnp.arange(slot_total, dtype=jnp.int32) < edge_count[0]
    dst_index = jnp.where(alive_slot, edge_dst, node_rows)
    adjacency = (
        jnp.zeros((node_rows + 1, table_rows), jnp.float32)
        .at[dst_index, edge_src]
        .add(1.0)[:node_rows]
    )
    degree = jnp.sum(adjacency, axis=1)
    floor_deg = jnp.maximum(degree, 1.0)[:, None]
    agg_sums = jnp.dot(adjacency, row_table.astype(jnp.float32), precision=lax.Precision.HIGHEST)
    aggregate = (agg_sums / floor_deg).astype(jnp.bfloat16)
    embedding = (
        jnp.dot(features, w_self, preferred_element_type=jnp.float32)
        + jnp.dot(aggregate, w_neigh, preferred_element_type=jnp.float32)
    ).astype(jnp.bfloat16)
    wanted = lax.all_to_all(
        request_rows[0], ("dom", "grp"), split_axis=0, concat_axis=0, tiled=True
    )
    req_len = wanted.shape[1]
    served = embedding[wanted]
    received = lax.all_to_all(served, ("dom", "grp"), split_axis=0, concat_axis=0, tiled=True)
    recv_rows = peer_count * req_len
    received = received.reshape(recv_rows, feat_width)
    slot_ids = jnp.arange(recv_rows, dtype=jnp.int32)[None, :]
    select_left = (pair_ends[:, 0][:, None] == slot_ids).astype(jnp.float32)
    select_right = (pair_ends[:, 1][:, None] == slot_ids).astype(jnp.float32)
    left_rows = jnp.dot(
        select_left.astype(jnp.bfloat16), received, preferred_element_type=jnp.float32
    ).astype(jnp.bfloat16)
    right_rows = jnp.dot(
        select_right.astype(jnp.bfloat16), received, preferred_element_type=jnp.float32
    ).astype(jnp.bfloat16)
    pair_input = jnp.concatenate([left_rows, right_rows], axis=1)
    pre_act = jnp.dot(pair_input, w_hidden, preferred_element_type=jnp.float32) + b_hidden
    hidden = jnp.maximum(pre_act, 0.0)
    logits = jnp.dot(hidden, w_out, precision=lax.Precision.HIGHEST)
    slope_term = pair_weight * (jax.nn.sigmoid(logits) - labels.astype(jnp.float32))
    grad_out = jnp.dot(slope_term, hidden, precision=lax.Precision.HIGHEST)
    delta_act = jnp.where(pre_act > 0, slope_term[:, None] * w_out[None, :], 0.0)
    grad_bias = jnp.sum(delta_act, axis=0)
    delta_b = delta_act.astype(jnp.bfloat16)
    grad_hidden = jnp.dot(pair_input.T, delta_b, preferred_element_type=jnp.float32)
    pair_grad = jnp.dot(delta_b, w_hidden.T, preferred_element_type=jnp.float32)
    received_grad = contract_rows(select_left, pair_grad[:, :feat_width]) + contract_rows(
        select_right, pair_grad[:, feat_width:]
    )
    received_grad_b = received_grad.astype(jnp.bfloat16)
    back_rows = lax.all_to_all(
        received_grad_b.reshape(peer_count, req_len, feat_width),
        ("dom", "grp"),
        split_axis=0,
        concat_axis=0,
        tiled=True,
    )
    embedding_grad = (
        jnp.zeros((node_rows, feat_width), jnp.float32)
        .at[wanted.reshape(recv_rows)]
        .add(back_rows.reshape(recv_rows, feat_width).astype(jnp.float32))
    )
    grad_b = embedding_grad.astype(jnp.bfloat16)
    grad_self = jnp.dot(features.T, grad_b, preferred_element_type=jnp.float32)
    grad_neigh = jnp.dot(aggregate.T, grad_b, preferred_element_type=jnp.float32)
    direct = jnp.dot(grad_b, w_self.T, preferred_element_type=jnp.float32)
    agg_grad = jnp.dot(grad_b, w_neigh.T, preferred_element_type=jnp.float32) / floor_deg
    table_grad = contract_rows(adjacency, agg_grad)
    returned = table_grad[node_rows:].reshape(peer_count, halo_len, feat_width)
    halo_back = lax.all_to_all(
        lax.all_to_all(
            returned.reshape(dom_count, grp_count, halo_len, feat_width).astype(jnp.bfloat16),
            "dom",
            split_axis=0,
            concat_axis=0,
            tiled=True,
        ),
        "grp",
        split_axis=1,
        concat_axis=1,
        tiled=True,
    ).astype(jnp.float32)
    grad_features = (
        (direct + table_grad[:node_rows])
        .at[halo_index[0].reshape(peer_count * halo_len)]
        .add(halo_back.reshape(peer_count * halo_len, feat_width))
    )
    summed = lax.psum((grad_self, grad_neigh, grad_hidden, grad_bias, grad_out), ("dom", "grp"))
    return (logits, grad_features, summed[0], summed[1], summed[2], summed[3], summed[4])


def solution(mesh):
    in_specs = (
        P(("dom", "grp"), None),
        P(("dom", "grp")),
        P(("dom", "grp")),
        P(("dom", "grp")),
        P(("dom", "grp"), None, None),
        P(("dom", "grp"), None, None),
        P(("dom", "grp"), None),
        P(("dom", "grp")),
        P(("dom", "grp")),
        P(),
        P(),
        P(),
        P(),
        P(),
    )
    out_specs = (P(("dom", "grp")), P(("dom", "grp"), None), P(), P(), P(), P(), P())
    return jax.shard_map(
        per_device, mesh=mesh, in_specs=in_specs, out_specs=out_specs, check_vma=False
    )
```

profile of v0, /device:TPU:0, one launch (start us, length us, event | category | flops | bytes accessed | tf_op | source)
XLA Modules:
  0.0 443.0 jit_solution(1680622156801528734)
XLA Ops:
  7.2 0.8 compare_select_fusion.4
  8.2 3.0 gather_fusion
  11.2 5.2 %all-to-all-start = ((bf16[8,4,8,256]{3,2,1,0:T(8,128)(2,1)}), bf16[8,4,8,256]{3,2,1,0:T(8,128)(2,1)S(1)}, u32[]{:S(2)}, u32[]{:S(2)}) async-start(bf16[8,4,8,256]{3,2,1,0:T(8,128)(2,1)} %bitcast.5), calls=%async_computation | async-start | bytes 262144 | tf_op jit(solution)/shard_map/all_to_all | solution.py:40
  17.0 0.9 compare_select_fusion
  17.9 0.9 compare_select_fusion.1
  18.7 0.9 multiply_reduce_fusion
  19.6 1.0 and_reduce_fusion
  20.6 0.6 broadcast_select_fusion
  21.2 1.3 fusion.50
  22.6 0.6 broadcast.84
  23.2 93.6 %scatter_custom_fusion.2 = f32[4720896]{0:T(1024)} fusion(s32[16384]{0:T(1024)} %broadcast_select_fusion, f32[16384]{0:T(1024)} %broadcast.84, f32[]{:T(128)} %constant.6.clone.1), kind=kCustom, calls=%fused_computation.5 | custom fusion | flops 16384 | bytes 18884096
  116.8 14.6 %slice.34 = f32[4718592]{0:T(1024)} slice(f32[4720896]{0:T(1024)} %scatter_custom_fusion.2), slice={[0:4718592]} | slice | bytes 37748736 | tf_op jit(solution)/shard_map/slice | solution.py:60
  131.4 20.7 %reshape.172 = f32[2048,2304]{1,0:T(8,128)} reshape(f32[4718592]{0:T(1024)} %slice.34) | data formatting | bytes 37748736 | tf_op jit(solution)/shard_map/slice | solution.py:60
  152.2 7.9 %reduce_sum.18 = f32[2048]{0:T(1024)} reduce(f32[2048,2304]{1,0:T(8,128)} %reshape.172, f32[]{:T(128)} %constant.6.clone.1), dimensions={1}, to_apply=%region_1.2 | reduce | flops 4716544 | bytes 18882564 | tf_op jit(solution)/shard_map/reduce_sum | solution.py:64
  160.0 0.7 copy.53
  160.7 6.3 %all-to-all-start.2 = ((s32[32,1,16]{2,1,0:T(1,128)}), s32[32,1,16]{2,1,0:T(1,128)S(1)}, u32[]{:S(2)}, u32[]{:S(2)}) async-start(s32[32,1,16]{2,1,0:T(1,128)} %bitcast.64), calls=%async_computation.2 | async-start | bytes 32768 | tf_op jit(solution)/shard_map/all_to_all | solution.py:72
  167.0 1.3 broadcast_maximum_fusion
  168.3 1.4 copy.54
  169.6 1.4 reshape_squeeze.3
  171.0 0.7 copy.51
  171.7 2.4 all-to-all-done.2
  174.1 3.8 all-to-all-start.1
  178.5 1.4 reshape.186
  179.9 1.3 pad_clamp_fusion
  181.2 2.8 all-to-all-done.1
  184.0 12.4 %fusion.5 = bf16[2048,256]{1,0:T(8,128)(2,1)S(1)} fusion(f32[2048,2304]{1,0:T(8,128)} %reshape.172, bf16[256,256]{1,0:T(8,128)(2,1)S(1)} %bitcast.58, bf16[2048,256]{1,0:T(8,128)(2,1)S(1)} %copy-done.1, f32[2048]{0:T(1024)} %broadcast_maximum_fusion), kind=kOutput, calls=%fused_computation.21 | convolution fusion | flops 14498922496 | bytes 21110784 | tf_op jit(solution)/shard_map/dot_general | solution.py:66
  196.4 1.0 copy-done.4
  197.8 2.8 gather_fusion.1
  200.7 3.1 all-to-all-start.3
  204.9 0.7 reduce.7
  205.6 8.3 %all-to-all-done.3 = bf16[32,16,256]{2,1,0:T(8,128)(2,1)S(1)} async-done(((bf16[32,16,256]{2,1,0:T(8,128)(2,1)}), bf16[32,16,256]{2,1,0:T(8,128)(2,1)S(1)}, u32[]{:S(2)}, u32[]{:S(2)}) %all-to-all-start.3) | async-done | bytes 262176 | tf_op jit(solution)/shard_map/all_to_all | solution.py:77
  214.0 1.3 convolution_convert_fusion
  215.3 1.5 convolution_convert_fusion.1
  216.8 0.8 convolution_add_fusion
  217.8 1.9 fusion.16
  219.7 0.6 copy-done.9
  220.3 1.1 fusion.8
  221.4 0.7 fusion.29
  222.2 3.8 fusion.2
  226.0 4.5 %fusion.22 = bf16[512,256]{1,0:T(8,128)(2,1)} fusion(f32[512,256]{1,0:T(8,128)S(1)} %fusion.2, f32[2048,512]{1,0:T(8,128)S(1)} %fusion.29, s32[2048]{0:T(1024)S(1)} %bitcast.69), kind=kOutput, calls=%fused_computation.38 | convolution fusion | flops 3222536192 | bytes 2891776 | tf_op jit(solution)/shard_map/dot_general | solution.py:8
  230.5 2.7 all-to-all-start.4
  233.2 3.2 fusion.18
  236.4 7.0 %all-to-all-done.4 = bf16[32,16,256]{2,1,0:T(8,128)(2,1)S(1)} async-done(((bf16[32,16,256]{2,1,0:T(8,128)(2,1)}), bf16[32,16,256]{2,1,0:T(8,128)(2,1)S(1)}, u32[]{:S(2)}, u32[]{:S(2)}) %all-to-all-start.4) | async-done | bytes 262176 | tf_op jit(solution)/shard_map/all_to_all | solution.py:104
  243.4 4.7 %scatter_custom_fusion = f32[2048,256]{1,0:T(8,128)} fusion(s32[512]{0:T(512)S(1)} %bitcast.74, f32[]{:T(128)} %constant.6.clone.1, bf16[512,256]{1,0:T(8,128)(2,1)S(1)} %bitcast.52), kind=kCustom, calls=%fused_computation.50 | custom fusion | flops 262144 | bytes 2359300 | tf_op jit(solution)/shard_map/scatter-add | solution.py:114
  248.2 1.8 convert_element_type.61
  250.0 1.2 fusion.52
  251.2 1.2 convolution_bitcast_fusion
  252.4 0.9 convolution_divide_fusion
  253.3 32.7 %fusion.51 = f32[2304,256]{1,0:T(8,128)S(1)} fusion(f32[2048,2304]{1,0:T(8,128)} %reshape.172, f32[2048,256]{1,0:T(8,128)S(1)} %convolution_divide_fusion), kind=kOutput, calls=%fused_computation.81 | convolution fusion | flops 14495514624 | bytes 23330816 | tf_op jit(solution)/shard_map/dot_general | solution.py:8
  286.0 1.4 copy-done.3
  287.4 0.7 slice.49
  288.1 3.4 all-to-all-start.5
  291.5 0.7 all-reduce.4.cloned.1.call-update
  292.2 1.0 fusion.14
  293.2 39.9 %all-reduce = (f32[256]{0:T(256)}, f32[256]{0:T(256)}) all-reduce(f32[256]{0:T(256)S(1)} %copy-done.16, f32[256]{0:T(256)S(1)} %bitcast.73), channel_id=1, replica_groups=mesh['dom'=8,'grp'=4] {'dom','grp'}, use_global_device_ids=true, to_apply=%region_8.9 | all-reduce | flops 512 | bytes 4096 | tf_op jit(solution)/shard_map/psum | solution.py:141
  333.1 0.7 copy.55
  333.8 3.3 all-to-all-start.6
  337.1 2.2 convolution_add_fusion.1
  339.3 4.0 all-to-all-done.6
  343.3 2.7 scatter_fusion
  346.1 84.3 %all-reduce.4.cloned.1.call-done = (f32[256,256]{0,1:T(8,128)}, f32[256,256]{1,0:T(8,128)}, f32[512,256]{1,0:T(8,128)}) async-done(((f32[256,256]{0,1:T(8,128)}, f32[256,256]{1,0:T(8,128)}, f32[512,256]{1,0:T(8,128)}), (f32[256,256]{0,1:T(8,128)}, f32[256,256]{1,0:T(8,128)}, f32[512,256]{1,0:T(8,128)})) %all-reduce.4.cloned.1.call-update) | async-done | bytes 1048592 | tf_op jit(solution)/shard_map/psum | solution.py:141
  430.4 1.8 copy.57
  432.2 1.7 copy.66
  433.9 1.9 copy.67
  (55 shorter events, 2.8 us)
Async XLA Ops:
  7.2 209.6 %copy-start = (bf16[512,256]{1,0:T(8,128)(2,1)S(1)}, bf16[512,256]{1,0:T(8,128)(2,1)}, u32[]{:S(2)}) copy-start(bf16[512,256]{1,0:T(8,128)(2,1)} %param.25) | copy-start | bytes 786436
  7.2 14.1 %copy-start.1 = (bf16[2048,256]{1,0:T(8,128)(2,1)S(1)}, bf16[2048,256]{1,0:T(8,128)(2,1)}, u32[]{:S(2)}) copy-start(bf16[2048,256]{1,0:T(8,128)(2,1)} %param.14) | copy-start | bytes 3145732
  11.2 149.6 %all-to-all-start = ((bf16[8,4,8,256]{3,2,1,0:T(8,128)(2,1)}), bf16[8,4,8,256]{3,2,1,0:T(8,128)(2,1)S(1)}, u32[]{:S(2)}, u32[]{:S(2)}) async-start(bf16[8,4,8,256]{3,2,1,0:T(8,128)(2,1)} %bitcast.5), calls=%async_computation | async-start | bytes 262144 | tf_op jit(solution)/shard_map/all_to_all | solution.py:40
  152.1 7.9 %copy-start.12 = (s32[1,32,16]{1,2,0:T(8,128)S(1)}, s32[1,32,16]{1,2,0:T(8,128)}, u32[]{:S(2)}) copy-start(s32[1,32,16]{1,2,0:T(8,128)} %param.19) | copy-start | bytes 6148
  160.7 13.4 %all-to-all-start.2 = ((s32[32,1,16]{2,1,0:T(1,128)}), s32[32,1,16]{2,1,0:T(1,128)S(1)}, u32[]{:S(2)}, u32[]{:S(2)}) async-start(s32[32,1,16]{2,1,0:T(1,128)} %bitcast.64), calls=%async_computation.2 | async-start | bytes 32768 | tf_op jit(solution)/shard_map/all_to_all | solution.py:72
  174.1 9.9 %all-to-all-start.1 = ((bf16[8,4,8,256]{3,2,0,1:T(8,128)(2,1)}), bf16[8,4,8,256]{3,2,0,1:T(8,128)(2,1)S(1)}, u32[]{:S(2)}, u32[]{:S(2)}) async-start(bf16[8,4,8,256]{3,2,0,1:T(8,128)(2,1)} %copy.51), calls=%async_computation.1 | async-start | bytes 262144 | tf_op jit(solution)/shard_map/all_to_all | solution.py:39
  184.0 13.4 %copy-start.7 = (bf16[256,256]{1,0:T(8,128)(2,1)S(1)}, bf16[256,256]{1,0:T(8,128)(2,1)}, u32[]{:S(2)}) copy-start(bf16[256,256]{1,0:T(8,128)(2,1)} %param.24) | copy-start | bytes 393220
  196.4 1.0 copy-start.4
  197.8 6.0 %copy-start.17 = (s32[256,1]{0,1:T(1,128)S(1)}, s32[256,1]{0,1:T(1,128)}, u32[]{:S(2)}) copy-start(s32[256,1]{0,1:T(1,128)} %reshape_squeeze.3) | copy-start | bytes 3076
  197.8 6.5 %copy-start.10 = (s32[2048,2]{0,1:T(2,128)S(1)}, s32[2048,2]{0,1:T(2,128)}, u32[]{:S(2)}) copy-start(s32[2048,2]{0,1:T(2,128)} %param.20) | copy-start | bytes 49156
  200.7 13.3 %all-to-all-start.3 = ((bf16[32,16,256]{2,1,0:T(8,128)(2,1)}), bf16[32,16,256]{2,1,0:T(8,128)(2,1)S(1)}, u32[]{:S(2)}, u32[]{:S(2)}) async-start(bf16[32,16,256]{2,1,0:T(8,128)(2,1)} %bitcast.9), calls=%async_computation.3 | async-start | bytes 524288 | tf_op jit(solution)/shard_map/all_to_all | solution.py:77
  215.3 1.5 copy-start.19
  215.3 1.5 copy-start.18
  216.8 1.0 copy-start.20
  216.8 1.0 copy-start.11
  217.8 2.5 copy-start.13
  217.8 2.5 copy-start.14
  219.7 0.6 copy-start.9
  230.5 12.9 %all-to-all-start.4 = ((bf16[32,16,256]{2,1,0:T(8,128)(2,1)}), bf16[32,16,256]{2,1,0:T(8,128)(2,1)S(1)}, u32[]{:S(2)}, u32[]{:S(2)}) async-start(bf16[32,16,256]{2,1,0:T(8,128)(2,1)} %bitcast.15), calls=%async_computation.4 | async-start | bytes 524288 | tf_op jit(solution)/shard_map/all_to_all | solution.py:104
  248.2 1.9 copy-start.5
  248.2 3.1 copy-start.2
  250.0 2.4 copy-start.8
  286.0 1.4 copy-start.3
  287.4 5.7 %copy-start.16 = (f32[256]{0:T(256)S(1)}, f32[256]{0:T(256)}, u32[]{:S(2)}) copy-start(f32[256]{0:T(256)} %get-tuple-element.54) | copy-start | bytes 3076
  288.1 45.0 %all-to-all-start.5 = ((bf16[8,4,8,256]{3,2,1,0:T(8,128)(2,1)}), bf16[8,4,8,256]{3,2,1,0:T(8,128)(2,1)S(1)}, u32[]{:S(2)}, u32[]{:S(2)}) async-start(bf16[8,4,8,256]{3,2,1,0:T(8,128)(2,1)} %bitcast.59), calls=%async_computation.5 | async-start | bytes 262144 | tf_op jit(solution)/shard_map/all_to_all | solution.py:124
  291.5 138.9 %all-reduce.4.cloned.1.call-start = ((), (), s32[]{:S(2)}) async-start(), calls=%async_computation.7 | async-start | bytes 2097152 | tf_op jit(solution)/shard_map/psum | solution.py:141
  333.8 9.5 %all-to-all-start.6 = ((bf16[8,4,8,256]{3,2,0,1:T(8,128)(2,1)}), bf16[8,4,8,256]{3,2,0,1:T(8,128)(2,1)S(1)}, u32[]{:S(2)}, u32[]{:S(2)}) async-start(bf16[8,4,8,256]{3,2,0,1:T(8,128)(2,1)} %copy.55), calls=%async_computation.6 | async-start | bytes 262144 | tf_op jit(solution)/shard_map/all_to_all | solution.py:123
  337.1 6.2 %copy-start.15 = (s32[256,1]{0,1:T(1,128)S(1)}, s32[256,1]{0,1:T(1,128)}, u32[]{:S(2)}) copy-start(s32[256,1]{0,1:T(1,128)} %compare_select_fusion.5) | copy-start | bytes 3076
  346.1 89.7 %copy-start.6 = (f32[2048,256]{1,0:T(8,128)}, f32[2048,256]{1,0:T(8,128)S(1)}, u32[]{:S(2)}) copy-start(f32[2048,256]{1,0:T(8,128)S(1)} %scatter_fusion) | copy-start | bytes 6291460
Sparse Core Ops, SparseCore 0:
  298.3 132.0 all-reduce.3
where the time goes:
time: 450 us; the launch traced here: 443 us
  other arithmetic  121 us (27%)
  waiting for transfers between devices  110 us (24%)
  matrix products  71 us (16%)
  local copies, waits for them, and re-layouts  58 us (13%)
  blocking collectives  39.9 us (9%)
  starting transfers between devices  27.7 us (6%)
  between operations  15.4 us (3%)
    unnamed x4, other arithmetic  96.1 us
    psum x1, waiting for transfers between devices, per_device(): lax.psum((grad_self, grad_neigh, grad_hidden, grad_bias, grad_out), ('dom...  84.3 us
    dot_general x3, matrix products, contract_rows(): lax.dot_general(left, right, (((0,), (0,)), ((), ())), precision=lax.Prec...  41 us
    psum x1, blocking collectives, per_device(): lax.psum((grad_self, grad_neigh, grad_hidden, grad_bias, grad_out), ('dom...  39.9 us
    slice x2, local copies, waits for them, and re-layouts, per_device(): jnp.zeros((node_rows + 1, table_rows), jnp.float32).at[dst_index, edge_src]  35.3 us
    dot_general x1, matrix products, per_device(): jnp.dot(adjacency, row_table.astype(jnp.float32), precision=lax.Precision...  12.4 us
    unnamed x48, local copies, waits for them, and re-layouts  11.3 us
  transfers between devices with their start and end apart: 8, of which 6 were waited for; matrix products, arithmetic and copies ran while one was open for 37% of the time, Pallas kernels for 0%

commit v1 on v0

v1 whole, which is shorter than its diff:
```python
import functools

import jax
import jax.numpy as jnp
from jax import lax
from jax.experimental import pallas as pl
from jax.experimental.pallas import tpu as pltpu
from jax.sharding import PartitionSpec as P

F32 = jnp.float32
BF16 = jnp.bfloat16
VMEM_LIMIT = 60 * 1024 * 1024
NN = (((1,), (0,)), ((), ()))
NT = (((1,), (1,)), ((), ()))
TN = (((0,), (0,)), ((), ()))


def dot(left, right, dims=NN):
    return lax.dot_general(left, right, dims, preferred_element_type=F32)


def column_of(row):
    return jnp.broadcast_to(row, (128, row.shape[1])).T[:, :1]


def row_of(column):
    return jnp.broadcast_to(column, (column.shape[0], 128)).T[:1, :]


def equal_mask(left, right):
    return jnp.where(left == right, 1.0, 0.0).astype(BF16)


def iota(shape, dim):
    return lax.broadcasted_iota(jnp.int32, shape, dim).astype(F32)


class Links:
    def __init__(self, peers, grp):
        self.peers, self.grp = peers, grp
        self.me = lax.axis_index("dom") * grp + lax.axis_index("grp")

    def device(self, peer):
        return {"dom": peer // self.grp, "grp": lax.rem(peer, self.grp)}

    def other(self, step):
        return lax.rem(self.me + step, self.peers)

    def each(self, body):
        def step(i, carry):
            body(self.other(i))
            return carry

        lax.fori_loop(1, self.peers, step, 0)

    def greet(self):
        barrier = pltpu.get_barrier_semaphore()
        self.each(lambda peer: pl.semaphore_signal(
            barrier, inc=1, device_id=self.device(peer), device_id_type=pl.DeviceIdType.MESH))

    def greeted(self):
        pl.semaphore_wait(pltpu.get_barrier_semaphore(), self.peers - 1)

    def copy(self, src, dst, send, recv, peer, slot):
        return pltpu.make_async_remote_copy(
            src_ref=src, dst_ref=dst, send_sem=send.at[peer], recv_sem=recv.at[slot],
            device_id=self.device(peer), device_id_type=pl.DeviceIdType.MESH)

    def start(self, moves):
        def one(peer):
            for pick, dst, send, recv in moves:
                self.copy(pick(peer), dst.at[self.me], send, recv, peer, self.me).start()

        self.each(one)

    def finish(self, moves):
        def one(peer):
            for pick, dst, send, recv in moves:
                copy = self.copy(pick(peer), dst.at[peer], send, recv, peer, peer)
                copy.wait_recv()
                copy.wait_send()

        self.each(one)


def block_of(ref):
    return lambda peer: ref.at[peer]


def whole_of(ref):
    return lambda peer: ref


def sems(peers, count):
    return [pltpu.SemaphoreType.DMA((peers,)) for _ in range(2 * count)]


def call(body, outs, args, scratch=(), collective_id=None, smem=()):
    params = dict(vmem_limit_bytes=VMEM_LIMIT)
    if collective_id is not None:
        params.update(collective_id=collective_id, has_side_effects=True)
    return pl.pallas_call(
        body,
        out_shape=tuple(jax.ShapeDtypeStruct(s, d) for s, d in outs),
        in_specs=[
            pl.BlockSpec(memory_space=pltpu.SMEM if i in smem else pltpu.VMEM)
            for i in range(len(args))
        ],
        out_specs=tuple(pl.BlockSpec(memory_space=pltpu.VMEM) for _ in outs),
        scratch_shapes=list(scratch),
        compiler_params=pltpu.CompilerParams(**params),
    )(*args)


def first_exchange(peers, grp, feat, halo_row, request, wanted, arrived, outgoing, s0, r0, s1, r1):
    links = Links(peers, grp)
    links.greet()
    halo_len, width = outgoing.shape[1:]
    nodes = feat.shape[0]
    index = column_of(halo_row[...].astype(F32))
    pick = equal_mask(index, iota((index.shape[0], nodes), 1))
    outgoing[...] = dot(pick, feat[...]).astype(BF16).reshape(outgoing.shape)
    links.greeted()
    moves = [(block_of(request), wanted, s0, r0), (block_of(outgoing), arrived, s1, r1)]
    links.start(moves)
    wanted[links.me] = request[links.me]
    arrived[links.me] = outgoing[links.me]
    links.finish(moves)


def swap_blocks(peers, grp, sent, got, s0, r0):
    links = Links(peers, grp)
    links.greet()
    links.greeted()
    moves = [(block_of(sent), got, s0, r0)]
    links.start(moves)
    got[links.me] = sent[links.me]
    links.finish(moves)


def swap_grads(peers, grp, rows, terms, small, got, got_terms, got_small, s0, r0, s1, r1, s2, r2):
    links = Links(peers, grp)
    links.greet()
    links.greeted()
    moves = [
        (block_of(rows), got, s0, r0),
        (block_of(terms), got_terms, s1, r1),
        (whole_of(small), got_small, s2, r2),
    ]
    links.start(moves)
    got[links.me] = rows[links.me]
    got_terms[links.me] = terms[links.me]
    got_small[links.me] = small[...]
    links.finish(moves)


def last_exchange(
    peers, grp, halo, terms_s, terms_n, in_hidden,
    got, all_s, all_n, all_h, in_s, in_n, own_s, own_n, own_h,
    s0, r0, s1, r1, s2, r2, s3, r3, s4, r4, s5, r5,
):
    links = Links(peers, grp)
    me = links.me
    links.greet()
    own_h[...] = jnp.sum(in_hidden[...].astype(F32), axis=0).astype(BF16)
    links.greeted()
    terms = [(block_of(terms_s), in_s, s1, r1), (block_of(terms_n), in_n, s2, r2)]
    late = [(block_of(halo), got, s0, r0), (whole_of(own_h), all_h, s5, r5)]
    links.start(terms)
    links.start(late)
    in_s[me] = terms_s[me]
    in_n[me] = terms_n[me]
    got[me] = halo[me]
    all_h[me] = own_h[...]
    links.finish(terms)
    own_s[...] = jnp.sum(in_s[...].astype(F32), axis=0).astype(BF16)
    own_n[...] = jnp.sum(in_n[...].astype(F32), axis=0).astype(BF16)
    sums = [(whole_of(own_s), all_s, s3, r3), (whole_of(own_n), all_n, s4, r4)]
    links.start(sums)
    all_s[me] = own_s[...]
    all_n[me] = own_n[...]
    links.finish(late)
    links.finish(sums)


def wanted_column(wanted, req_len):
    peers = wanted.shape[0]
    spread = jnp.broadcast_to(wanted[...].astype(F32), (peers, req_len, 128)).reshape(peers * req_len, 128)
    lane = lax.broadcasted_iota(jnp.int32, spread.shape, 1)
    row = lax.rem(lax.broadcasted_iota(jnp.int32, spread.shape, 0), req_len)
    return jnp.sum(jnp.where(lane == row, spread, 0.0), axis=1, keepdims=True)


def count_edges(req_len, chunk, block, src, dst, count, wanted, counts, total, marks, ladder):
    rows, table_rows = counts.shape
    slots = src.shape[1]
    total[...] = jnp.zeros_like(total)
    index = wanted_column(wanted, req_len)
    ladder[...] = iota(ladder.shape, 0).astype(BF16)

    @pl.loop(0, slots // chunk)
    def _(c):
        span = pl.ds(pl.multiple_of(c * chunk, chunk), chunk)
        place = lax.broadcasted_iota(jnp.int32, (1, chunk), 1) + c * chunk
        into = jnp.where(place < count[0], dst[:, span], -1).astype(F32)
        marks[...] = equal_mask(index, into)
        source = src[:, span]
        high = source // block
        low = lax.rem(source, block)

        @pl.loop(0, table_rows // block)
        def _(b):
            here = jnp.where(high == b, low, -1).astype(F32).astype(BF16)
            hit = jnp.where(ladder[...] == here, jnp.array(1, BF16), jnp.array(0, BF16))
            cols = pl.ds(pl.multiple_of(b * block, block), block)
            total[:, cols] += dot(marks[...], hit, NT)

    counts[...] = total[...].astype(BF16)


def encode(req_len, block, feat, arrived, counts, wanted, w_self, w_neigh, served, feat_w, agg_w, floor):
    nodes, width = feat.shape
    rows, table_rows = counts.shape
    peers, halo_len = arrived.shape[:2]
    index = wanted_column(wanted, req_len)
    degree = jnp.sum(counts[...].astype(F32), axis=1, keepdims=True)
    floor_deg = jnp.maximum(degree, 1.0)
    sums = dot(counts[:, :nodes], feat[...])
    sums += dot(counts[:, nodes:], arrived[...].reshape(peers * halo_len, width))
    agg = (sums / floor_deg).astype(BF16)
    pick = equal_mask(index, iota((rows, nodes), 1))
    own = dot(pick, feat[...]).astype(BF16)
    emb = (dot(own, w_self[...]) + dot(agg, w_neigh[...])).astype(BF16)
    served[...] = emb.reshape(served.shape)
    feat_w[...] = own
    agg_w[...] = agg
    floor[...] = jnp.broadcast_to(floor_deg, floor.shape)


def encode_back(
    req_len, block, back, wanted, counts, feat_w, agg_w, floor, w_self, w_neigh,
    local, returned, grad_self, grad_neigh, near, far,
):
    nodes, width = local.shape
    rows, table_rows = counts.shape
    index = wanted_column(wanted, req_len)
    other = row_of(index)
    same = index == other
    earlier = lax.broadcasted_iota(jnp.int32, (rows, rows), 1) < lax.broadcasted_iota(jnp.int32, (rows, rows), 0)
    seen = jnp.sum(jnp.where(same & earlier, 1.0, 0.0), axis=1, keepdims=True)
    grad = dot(jnp.where(same, 1.0, 0.0).astype(BF16), back[...].reshape(rows, width))
    grad = jnp.where(seen > 0.0, 0.0, grad).astype(BF16)
    grad_self[...] = dot(feat_w[...], grad, TN).astype(BF16).reshape(grad_self.shape)
    grad_neigh[...] = dot(agg_w[...], grad, TN).astype(BF16).reshape(grad_neigh.shape)
    near[...] = dot(grad, w_self[...], NT).astype(BF16)
    far[...] = (dot(grad, w_neigh[...], NT) / floor[:, :1]).astype(BF16)

    @pl.loop(0, nodes // block)
    def _(b):
        cols = pl.ds(pl.multiple_of(b * block, block), block)
        spot = lax.broadcasted_iota(jnp.int32, (1, block), 1) + b * block
        pick = equal_mask(index, spot.astype(F32))
        local[cols, :] = dot(counts[:, cols], far[...], TN) + dot(pick, near[...], TN)

    halo = dot(counts[:, nodes:], far[...], TN)
    returned[...] = halo.astype(BF16).reshape(returned.shape)


def decode(
    chunk, received, ends, labels, weight, w_hidden, bias, w_out,
    logits, back, grad_hidden, small, picks, left_right, sums,
):
    peers, req_len, width = received.shape
    rows = peers * req_len
    got = received[...].reshape(rows, width)
    for place, half in ((0, w_hidden[:width, :]), (rows, w_hidden[width:, :])):
        exact = dot(got, half).T
        upper = exact.astype(BF16)
        left_right[0, :, place : place + rows] = upper
        left_right[1, :, place : place + rows] = (exact - upper.astype(F32)).astype(BF16)
    bias_col = column_of(bias[...])
    out_col = column_of(w_out[...])
    sums[...] = jnp.zeros_like(sums)
    slots = iota((rows, chunk), 0)

    def step(c, carry):
        bias_sum, out_sum = carry
        span = pl.ds(pl.multiple_of(c * chunk, chunk), chunk)
        end = ends[:, span].astype(F32)
        picks[:rows, :] = equal_mask(slots, end[:1, :])
        picks[rows:, :] = equal_mask(slots, end[1:, :])
        pre = dot(left_right[0], picks[...]) + dot(left_right[1], picks[...]) + bias_col
        hidden = jnp.maximum(pre, 0.0)
        logit = jnp.sum(hidden * out_col, axis=0, keepdims=True)
        logits[:, span] = logit
        slope = weight[:, span] * (jax.nn.sigmoid(logit) - labels[:, span].astype(F32))
        delta = jnp.where(pre > 0, slope * out_col, 0.0)
        sums[...] += dot(picks[...], delta.astype(BF16), NT)
        return (
            bias_sum + jnp.sum(delta, axis=1, keepdims=True),
            out_sum + jnp.sum(hidden * slope, axis=1, keepdims=True),
        )

    zero = jnp.zeros((width, 1), F32)
    bias_sum, out_sum = lax.fori_loop(0, ends.shape[1] // chunk, step, (zero, zero))
    small[0:1, :] = row_of(bias_sum)
    small[1:2, :] = row_of(out_sum)
    left = sums[:rows, :].astype(BF16)
    right = sums[rows:, :].astype(BF16)
    half = grad_hidden.shape[0] // 2
    shape = (half,) + grad_hidden.shape[1:]
    grad_hidden[:half] = dot(got, left, TN).astype(BF16).reshape(shape)
    grad_hidden[half:] = dot(got, right, TN).astype(BF16).reshape(shape)
    back_rows = dot(left, w_hidden[:width, :], NT) + dot(right, w_hidden[width:, :], NT)
    back[...] = back_rows.astype(BF16).reshape(back.shape)


def finish(local, halo_back, halo_row, in_s, in_n, in_h, in_small, out, g_s, g_n, g_h, g_b, g_o):
    nodes, width = local.shape
    rows = halo_row.shape[1]
    pick = equal_mask(iota((nodes, rows), 0), halo_row[...].astype(F32))
    out[...] = local[...] + dot(pick, halo_back[...].reshape(rows, width))
    g_s[...] = in_s[...].astype(F32).reshape(g_s.shape)
    g_n[...] = in_n[...].astype(F32).reshape(g_n.shape)
    g_h[...] = in_h[...].astype(F32).reshape(g_h.shape)
    small = jnp.sum(in_small[...], axis=0)
    g_b[...] = small[0:1, :]
    g_o[...] = small[1:2, :]


def per_device(
    features, edge_src, edge_dst, edge_count, halo_index, request_rows, pair_ends,
    labels, pair_weight, w_self, w_neigh, w_hidden, b_hidden, w_out,
):
    nodes, width = features.shape
    grp = lax.axis_size("grp")
    peers = lax.axis_size("dom") * grp
    halo_len = halo_index.shape[2]
    req_len = request_rows.shape[2]
    slots = edge_src.shape[0]
    pairs = labels.shape[0]
    table_rows = nodes + peers * halo_len
    rows = peers * req_len
    block = 256
    part = width // peers
    hidden_part = 2 * width // peers

    halo_row = halo_index.reshape(1, peers * halo_len)
    request = jnp.pad(request_rows[0], ((0, 0), (0, 128 - req_len))).reshape(peers, 1, 128)
    wanted, arrived = call(
        functools.partial(first_exchange, peers, grp),
        [((peers, 1, 128), jnp.int32), ((peers, halo_len, width), BF16)],
        (features, halo_row, request),
        [pltpu.VMEM((peers, halo_len, width), BF16)] + sems(peers, 2),
        collective_id=0,
    )
    edge_chunk = 2048
    (counts,) = call(
        functools.partial(count_edges, req_len, edge_chunk, block),
        [((rows, table_rows), BF16)],
        (edge_src.reshape(1, slots), edge_dst.reshape(1, slots), edge_count, wanted),
        [
            pltpu.VMEM((rows, table_rows), F32),
            pltpu.VMEM((rows, edge_chunk), BF16),
            pltpu.VMEM((block, edge_chunk), BF16),
        ],
        smem=(2,),
    )
    served, feat_w, agg_w, floor = call(
        functools.partial(encode, req_len, block),
        [
            ((peers, req_len, width), BF16),
            ((rows, width), BF16),
            ((rows, width), BF16),
            ((rows, 128), F32),
        ],
        (features, arrived, counts, wanted, w_self, w_neigh),
    )
    (received,) = call(
        functools.partial(swap_blocks, peers, grp),
        [((peers, req_len, width), BF16)],
        (served,),
        sems(peers, 1),
        collective_id=1,
    )
    pair_chunk = 512
    logits, back_sent, hidden_terms, small = call(
        functools.partial(decode, pair_chunk),
        [
            ((1, pairs), F32),
            ((peers, req_len, width), BF16),
            ((peers, hidden_part, width), BF16),
            ((2, width), F32),
        ],
        (
            received, pair_ends.T, labels.reshape(1, pairs), pair_weight.reshape(1, pairs),
            w_hidden, b_hidden.reshape(1, width), w_out.reshape(1, width),
        ),
        [
            pltpu.VMEM((2 * rows, pair_chunk), BF16),
            pltpu.VMEM((2, width, 2 * rows), BF16),
            pltpu.VMEM((2 * rows, width), F32),
        ],
    )
    back, in_hidden, in_small = call(
        functools.partial(swap_grads, peers, grp),
        [
            ((peers, req_len, width), BF16),
            ((peers, hidden_part, width), BF16),
            ((peers, 2, width), F32),
        ],
        (back_sent, hidden_terms, small),
        sems(peers, 3),
        collective_id=2,
    )
    local, returned, terms_s, terms_n = call(
        functools.partial(encode_back, req_len, block),
        [
            ((nodes, width), F32),
            ((peers, halo_len, width), BF16),
            ((peers, part, width), BF16),
            ((peers, part, width), BF16),
        ],
        (back, wanted, counts, feat_w, agg_w, floor, w_self, w_neigh),
        [pltpu.VMEM((rows, width), BF16), pltpu.VMEM((rows, width), BF16)],
    )
    halo_back, all_s, all_n, all_h = call(
        functools.partial(last_exchange, peers, grp),
        [
            ((peers, halo_len, width), BF16),
            ((peers, part, width), BF16),
            ((peers, part, width), BF16),
            ((peers, hidden_part, width), BF16),
        ],
        (returned, terms_s, terms_n, in_hidden),
        [
            pltpu.VMEM((peers, part, width), BF16),
            pltpu.VMEM((peers, part, width), BF16),
            pltpu.VMEM((part, width), BF16),
            pltpu.VMEM((part, width), BF16),
            pltpu.VMEM((hidden_part, width), BF16),
        ] + sems(peers, 6),
        collective_id=3,
    )
    grad_features, g_s, g_n, g_h, g_b, g_o = call(
        finish,
        [
            ((nodes, width), F32),
            ((width, width), F32),
            ((width, width), F32),
            ((2 * width, width), F32),
            ((1, width), F32),
            ((1, width), F32),
        ],
        (local, halo_back, halo_row, all_s, all_n, all_h, in_small),
    )
    return (logits.reshape(pairs), grad_features, g_s, g_n, g_h, g_b.reshape(width), g_o.reshape(width))


def solution(mesh):
    both = ("dom", "grp")
    in_specs = (
        P(both, None), P(both), P(both), P(both), P(both, None, None), P(both, None, None),
        P(both, None), P(both), P(both), P(), P(), P(), P(), P(),
    )
    out_specs = (P(both), P(both, None), P(), P(), P(), P(), P())
    return jax.shard_map(
        per_device, mesh=mesh, in_specs=in_specs, out_specs=out_specs, check_vma=False
    )
```

time: 450 us -> 170 us (0.38); the launches traced: 443 us -> 170 us
  Pallas kernels: 0 us -> 166 us
  other arithmetic: 121 us -> 0 us
  waiting for transfers between devices: 110 us -> 0 us
  matrix products: 71 us -> 0 us
  local copies, waits for them, and re-layouts: 58 us -> 2.81 us
  blocking collectives: 39.9 us -> 0 us
  starting transfers between devices: 27.7 us -> 0 us
  between operations: 15.4 us -> 1.31 us
    pallas_call x0 -> x9, Pallas kernels: none -> 166 us  [call(): pl.pallas_call(body, out_shape=tuple((jax.ShapeDtypeStruct(s, d) for s, d...]
    unnamed x4 -> x0, other arithmetic: 96.1 us -> none
    psum x1 -> x0, waiting for transfers between devices: 84.3 us -> none  [per_device(): lax.psum((grad_self, grad_neigh, grad_hidden, grad_bias, grad_out), ('dom...]
    dot_general x17 -> x0, matrix products: 71 us -> none  [the longest x3 41 us: contract_rows(): lax.dot_general(left, right, (((0,), (0,)), ((), ())), precision=lax.Prec...]
    psum x1 -> x0, blocking collectives: 39.9 us -> none  [per_device(): lax.psum((grad_self, grad_neigh, grad_hidden, grad_bias, grad_out), ('dom...]
    slice x4 -> x0, local copies, waits for them, and re-layouts: 36 us -> none  [the longest x2 35.3 us: per_device(): jnp.zeros((node_rows + 1, table_rows), jnp.float32).at[dst_index, edge_src]]
    all_to_all x7 -> x0, starting transfers between devices: 27.7 us -> none  [the longest x1 6.25 us: per_device(): lax.all_to_all(request_rows[0], ('dom', 'grp'), split_axis=0, concat_axis...]
    all_to_all x7 -> x0, waiting for transfers between devices: 24.6 us -> none  [the longest x1 8.33 us: per_device(): lax.all_to_all(served, ('dom', 'grp'), split_axis=0, concat_axis=0, tiled...]
  transfers between devices with their start and end apart: 8 -> 0, of which waited for: 6 -> 0; matrix products, arithmetic and copies ran while one was open for 37% -> 0% of each run, Pallas kernels for 0% -> 0%
where the time goes in v1:
time: 170 us
  Pallas kernels  166 us (98%)
  local copies, waits for them, and re-layouts  2.81 us (2%)
    pallas_call x9, Pallas kernels, call(): pl.pallas_call(body, out_shape=tuple((jax.ShapeDtypeStruct(s, d) for s, d...  166 us

profile of v1, /device:TPU:0, one launch (start us, length us, event | category | flops | bytes accessed | tf_op | source)
XLA Modules:
  0.0 169.9 jit_solution(17740975158562257418)
XLA Ops:
  1.3 0.8 copy.23
  2.0 0.7 reshape.47.halo_row
  2.7 0.8 copy.24
  3.5 0.6 pad.4
  4.1 15.0 %shard_map.189 = (s32[32,1,128]{2,1,0:T(1,128)}, bf16[32,8,256]{2,1,0:T(8,128)(2,1)}) custom-call(bf16[2048,256]{1,0:T(8,128)(2,1)} %feat.3, s32[1,256]{1,0:T(1,128)} %reshape.47.halo_row, s32[32,1,128]{2,1,0:T(1,128)} %bitcast.12), custom_call_target="tpu_custom_call" | custom-call | tf_op jit(solution)/shard_map/pallas_call | solution.py:102
  19.1 60.3 %shard_map.190.counts = bf16[512,2304]{1,0:T(8,128)(2,1)} custom-call(s32[1,16384]{1,0:T(1,128)} %bitcast.13, s32[1,16384]{1,0:T(1,128)} %bitcast.14, s32[1]{0:T(128)S(6)} %copy.25.count, s32[32,1,128]{2,1,0:T(1,128)} %get-tuple-element.35.wanted), custom_call_target="tpu_custom_call" | custom-call | tf_op jit(solution)/shard_map/pallas_call | solution.py:102
  79.4 4.6 %shard_map.191 = (bf16[32,16,256]{2,1,0:T(8,128)(2,1)}, bf16[512,256]{1,0:T(8,128)(2,1)}, bf16[512,256]{1,0:T(8,128)(2,1)}, f32[512,128]{1,0:T(8,128)}) custom-call(bf16[2048,256]{1,0:T(8,128)(2,1)} %feat.3, bf16[32,8,256]{2,1,0:T(8,128)(2,1)} %get-tuple-element.34.arrived, bf16[512,2304]{1,0:T(8,128)(2,1)} %shard_map.190.counts, ...), custom_call_target="tpu_custom_call" | custom-call | tf_op jit(solution)/shard_map/pallas_call | solution.py:102
  84.0 13.7 %shard_map.192.received = bf16[32,16,256]{2,1,0:T(8,128)(2,1)} custom-call(bf16[32,16,256]{2,1,0:T(8,128)(2,1)} %get-tuple-element.36.sent), custom_call_target="tpu_custom_call" | custom-call | tf_op jit(solution)/shard_map/pallas_call | solution.py:102
  97.6 8.3 %shard_map.193 = (f32[1,2048]{1,0:T(1,128)}, bf16[32,16,256]{2,1,0:T(8,128)(2,1)}, bf16[32,16,256]{2,1,0:T(8,128)(2,1)}, f32[2,256]{1,0:T(2,128)}) custom-call(bf16[32,16,256]{2,1,0:T(8,128)(2,1)} %shard_map.192.received, s32[2,2048]{1,0:T(2,128)} %bitcast.16, s32[1,2048]{1,0:T(1,128)} %bitcast.17, f32[1,2048]{1,0:T(1,128)} %bitcast.18, ...), custom_call_target="tpu_custom_call" | custom-call | tf_op jit(solution)/shard_map/pallas_call | solution.py:102
  105.9 22.0 %shard_map.194 = (bf16[32,16,256]{2,1,0:T(8,128)(2,1)}, bf16[32,16,256]{2,1,0:T(8,128)(2,1)}, f32[32,2,256]{2,1,0:T(2,128)}) custom-call(bf16[32,16,256]{2,1,0:T(8,128)(2,1)} %get-tuple-element.38.rows, bf16[32,16,256]{2,1,0:T(8,128)(2,1)} %get-tuple-element.39.terms, f32[2,256]{1,0:T(2,128)} %get-tuple-element.40.small), custom_call_target="tpu_custom_call" | custom-call | tf_op jit(solution)/shard_map/pallas_call | solution.py:102
  128.0 7.2 %shard_map.195 = (f32[2048,256]{1,0:T(8,128)}, bf16[32,8,256]{2,1,0:T(8,128)(2,1)}, bf16[32,8,256]{2,1,0:T(8,128)(2,1)}, bf16[32,8,256]{2,1,0:T(8,128)(2,1)}) custom-call(bf16[32,16,256]{2,1,0:T(8,128)(2,1)} %get-tuple-element.41.back, s32[32,1,128]{2,1,0:T(1,128)} %get-tuple-element.35.wanted, bf16[512,2304]{1,0:T(8,128)(2,1)} %shard_map.190.counts, ...), custom_call_target="tpu_custom_call" | custom-call | tf_op jit(solution)/shard_map/pallas_call | solution.py:102
  135.2 30.8 %shard_map.196 = (bf16[32,8,256]{2,1,0:T(8,128)(2,1)}, bf16[32,8,256]{2,1,0:T(8,128)(2,1)}, bf16[32,8,256]{2,1,0:T(8,128)(2,1)}, bf16[32,16,256]{2,1,0:T(8,128)(2,1)}) custom-call(bf16[32,8,256]{2,1,0:T(8,128)(2,1)} %get-tuple-element.46.halo, bf16[32,8,256]{2,1,0:T(8,128)(2,1)} %get-tuple-element.47.terms_s, bf16[32,8,256]{2,1,0:T(8,128)(2,1)} %get-tuple-element.48.terms_n, ...), custom_call_target="tpu_custom_call" | custom-call | tf_op jit(solution)/shard_map/pallas_call | solution.py:102
  166.1 3.9 %shard_map.197 = (f32[2048,256]{1,0:T(8,128)}, f32[256,256]{1,0:T(8,128)}, f32[256,256]{1,0:T(8,128)}, f32[512,256]{1,0:T(8,128)}, f32[1,256]{1,0:T(1,128)}, /*index=5*/f32[1,256]{1,0:T(1,128)}) custom-call(f32[2048,256]{1,0:T(8,128)} %get-tuple-element.45.local, bf16[32,8,256]{2,1,0:T(8,128)(2,1)} %get-tuple-element.50.halo_back, ...), custom_call_target="tpu_custom_call" | custom-call | tf_op jit(solution)/shard_map/pallas_call | solution.py:102

commit v2 on v1

--- a/solution.py
+++ b/solution.py
@@ -9,6 +9,7 @@
 
 F32 = jnp.float32
 BF16 = jnp.bfloat16
+F8 = jnp.float8_e4m3fn
 VMEM_LIMIT = 60 * 1024 * 1024
 NN = (((1,), (0,)), ((), ()))
 NT = (((1,), (1,)), ((), ()))
@@ -203,7 +204,7 @@
         span = pl.ds(pl.multiple_of(c * chunk, chunk), chunk)
         place = lax.broadcasted_iota(jnp.int32, (1, chunk), 1) + c * chunk
         into = jnp.where(place < count[0], dst[:, span], -1).astype(F32)
-        marks[...] = equal_mask(index, into)
+        marks[...] = jnp.where(index == into, 1.0, 0.0).astype(F8)
         source = src[:, span]
         high = source // block
         low = lax.rem(source, block)
@@ -211,7 +212,7 @@
         @pl.loop(0, table_rows // block)
         def _(b):
             here = jnp.where(high == b, low, -1).astype(F32).astype(BF16)
-            hit = jnp.where(ladder[...] == here, jnp.array(1, BF16), jnp.array(0, BF16))
+            hit = jnp.where(ladder[...] == here, jnp.array(1, BF16), jnp.array(0, BF16)).astype(F8)
             cols = pl.ds(pl.multiple_of(b * block, block), block)
             total[:, cols] += dot(marks[...], hit, NT)
 
@@ -361,7 +362,7 @@
         (edge_src.reshape(1, slots), edge_dst.reshape(1, slots), edge_count, wanted),
         [
             pltpu.VMEM((rows, table_rows), F32),
-            pltpu.VMEM((rows, edge_chunk), BF16),
+            pltpu.VMEM((rows, edge_chunk), F8),
             pltpu.VMEM((block, edge_chunk), BF16),
         ],
         smem=(2,),

time: 170 us -> 147 us (0.86)
  Pallas kernels: 166 us -> 143 us
    pallas_call x9, Pallas kernels: 166 us -> 143 us  [call(): pl.pallas_call(body, out_shape=tuple((jax.ShapeDtypeStruct(s, d) for s, d...]
where the time goes in v2:
time: 147 us
  Pallas kernels  143 us (97%)
  local copies, waits for them, and re-layouts  2.81 us (2%)
    pallas_call x9, Pallas kernels, call(): pl.pallas_call(body, out_shape=tuple((jax.ShapeDtypeStruct(s, d) for s, d...  143 us

profile of v2, /device:TPU:0, one launch (start us, length us, event | category | flops | bytes accessed | tf_op | source)
XLA Modules:
  0.0 146.9 jit_solution(8536047678827658916)
XLA Ops:
  1.3 0.8 copy.23
  2.0 0.7 reshape.47.halo_row
  2.7 0.8 copy.24
  3.5 0.6 pad.4
  4.1 15.0 %shard_map.189 = (s32[32,1,128]{2,1,0:T(1,128)}, bf16[32,8,256]{2,1,0:T(8,128)(2,1)}) custom-call(bf16[2048,256]{1,0:T(8,128)(2,1)} %feat.3, s32[1,256]{1,0:T(1,128)} %reshape.47.halo_row, s32[32,1,128]{2,1,0:T(1,128)} %bitcast.12), custom_call_target="tpu_custom_call" | custom-call | tf_op jit(solution)/shard_map/pallas_call | solution.py:103
  19.1 37.2 %shard_map.190.counts = bf16[512,2304]{1,0:T(8,128)(2,1)} custom-call(s32[1,16384]{1,0:T(1,128)} %bitcast.13, s32[1,16384]{1,0:T(1,128)} %bitcast.14, s32[1]{0:T(128)S(6)} %copy.25.count, s32[32,1,128]{2,1,0:T(1,128)} %get-tuple-element.35.wanted), custom_call_target="tpu_custom_call" | custom-call | tf_op jit(solution)/shard_map/pallas_call | solution.py:103
  56.3 4.6 %shard_map.191 = (bf16[32,16,256]{2,1,0:T(8,128)(2,1)}, bf16[512,256]{1,0:T(8,128)(2,1)}, bf16[512,256]{1,0:T(8,128)(2,1)}, f32[512,128]{1,0:T(8,128)}) custom-call(bf16[2048,256]{1,0:T(8,128)(2,1)} %feat.3, bf16[32,8,256]{2,1,0:T(8,128)(2,1)} %get-tuple-element.34.arrived, bf16[512,2304]{1,0:T(8,128)(2,1)} %shard_map.190.counts, ...), custom_call_target="tpu_custom_call" | custom-call | tf_op jit(solution)/shard_map/pallas_call | solution.py:103
  60.9 13.7 %shard_map.192.received = bf16[32,16,256]{2,1,0:T(8,128)(2,1)} custom-call(bf16[32,16,256]{2,1,0:T(8,128)(2,1)} %get-tuple-element.36.sent), custom_call_target="tpu_custom_call" | custom-call | tf_op jit(solution)/shard_map/pallas_call | solution.py:103
  74.6 8.3 %shard_map.193 = (f32[1,2048]{1,0:T(1,128)}, bf16[32,16,256]{2,1,0:T(8,128)(2,1)}, bf16[32,16,256]{2,1,0:T(8,128)(2,1)}, f32[2,256]{1,0:T(2,128)}) custom-call(bf16[32,16,256]{2,1,0:T(8,128)(2,1)} %shard_map.192.received, s32[2,2048]{1,0:T(2,128)} %bitcast.16, s32[1,2048]{1,0:T(1,128)} %bitcast.17, f32[1,2048]{1,0:T(1,128)} %bitcast.18, ...), custom_call_target="tpu_custom_call" | custom-call | tf_op jit(solution)/shard_map/pallas_call | solution.py:103
  82.9 22.0 %shard_map.194 = (bf16[32,16,256]{2,1,0:T(8,128)(2,1)}, bf16[32,16,256]{2,1,0:T(8,128)(2,1)}, f32[32,2,256]{2,1,0:T(2,128)}) custom-call(bf16[32,16,256]{2,1,0:T(8,128)(2,1)} %get-tuple-element.38.rows, bf16[32,16,256]{2,1,0:T(8,128)(2,1)} %get-tuple-element.39.terms, f32[2,256]{1,0:T(2,128)} %get-tuple-element.40.small), custom_call_target="tpu_custom_call" | custom-call | tf_op jit(solution)/shard_map/pallas_call | solution.py:103
  104.9 7.2 %shard_map.195 = (f32[2048,256]{1,0:T(8,128)}, bf16[32,8,256]{2,1,0:T(8,128)(2,1)}, bf16[32,8,256]{2,1,0:T(8,128)(2,1)}, bf16[32,8,256]{2,1,0:T(8,128)(2,1)}) custom-call(bf16[32,16,256]{2,1,0:T(8,128)(2,1)} %get-tuple-element.41.back, s32[32,1,128]{2,1,0:T(1,128)} %get-tuple-element.35.wanted, bf16[512,2304]{1,0:T(8,128)(2,1)} %shard_map.190.counts, ...), custom_call_target="tpu_custom_call" | custom-call | tf_op jit(solution)/shard_map/pallas_call | solution.py:103
  112.1 30.8 %shard_map.196 = (bf16[32,8,256]{2,1,0:T(8,128)(2,1)}, bf16[32,8,256]{2,1,0:T(8,128)(2,1)}, bf16[32,8,256]{2,1,0:T(8,128)(2,1)}, bf16[32,16,256]{2,1,0:T(8,128)(2,1)}) custom-call(bf16[32,8,256]{2,1,0:T(8,128)(2,1)} %get-tuple-element.46.halo, bf16[32,8,256]{2,1,0:T(8,128)(2,1)} %get-tuple-element.47.terms_s, bf16[32,8,256]{2,1,0:T(8,128)(2,1)} %get-tuple-element.48.terms_n, ...), custom_call_target="tpu_custom_call" | custom-call | tf_op jit(solution)/shard_map/pallas_call | solution.py:103
  143.0 3.9 %shard_map.197 = (f32[2048,256]{1,0:T(8,128)}, f32[256,256]{1,0:T(8,128)}, f32[256,256]{1,0:T(8,128)}, f32[512,256]{1,0:T(8,128)}, f32[1,256]{1,0:T(1,128)}, /*index=5*/f32[1,256]{1,0:T(1,128)}) custom-call(f32[2048,256]{1,0:T(8,128)} %get-tuple-element.45.local, bf16[32,8,256]{2,1,0:T(8,128)(2,1)} %get-tuple-element.50.halo_back, ...), custom_call_target="tpu_custom_call" | custom-call | tf_op jit(solution)/shard_map/pallas_call | solution.py:103
